TPU v7x, 32 devices: a whole 2x2x4 slice. The times are simulated.
32 devices in a mesh: section: 2 (over core), tensor: 2 (over x), dp: 8 (over z, y).
Axes of the slice: x: 2, y: 2, z: 4, core: 2. Of those that a mesh axis runs over, the one named last changes fastest.
Arguments:
- exit_hidden: bfloat16 [64, 4, 2048], P('dp', None, ('section', 'tensor')), may hold values from -6 to 6
- exit_depth: int32 [64], P('dp'), may hold values from 0 to 1, as said below
- context_len: int32 [64], P('dp'), may hold values from 48 to 384
- attn_gain: float32 [2, 2048], P('section'), may hold values from 0.1 to 1.9
- w_query: bfloat16 [2, 2048, 2048], P('section', None, 'tensor'), may hold values from -0.125 to 0.125
- w_keyval: bfloat16 [2, 2048, 1024], P('section', None, 'tensor'), may hold values from -0.125 to 0.125
- w_out: bfloat16 [2, 2048, 2048], P('section', 'tensor'), may hold values from -0.125 to 0.125
- kv_cache: bfloat16 [2, 64, 384, 8, 128], P('section', 'dp', None, 'tensor'), may hold values from -400 to 400
- mlp_gain: float32 [2, 2048], P('section'), may hold values from 0.1 to 1.9
- w_gate: bfloat16 [2, 2048, 4096], P('section', 'dp', 'tensor'), may hold values from -0.125 to 0.125
- w_up: bfloat16 [2, 2048, 4096], P('section', 'dp', 'tensor'), may hold values from -0.125 to 0.125
- w_down: bfloat16 [2, 2048, 4096], P('section', 'dp', 'tensor'), may hold values from -0.09375 to 0.09375
Outputs:
- layer_states: bfloat16 [2, 64, 4, 2048], P('section', 'dp', None, 'tensor')
Inputs may be any that keep to these rules, and one draw needn't show every extreme that they name: `exit_depth`: every depth from 0 to 1 is held by some request.
All inputs are finite; a program needn't handle non-finite values.
Results may differ from a plain program's by a relative error of at most 0.019.
Values may be sent and summed in bfloat16 or wider, within the bound.
A program may use at most 192 MiB of HBM per device.

v0:
```python
import math
import jax
import jax.numpy as jnp
from jax import lax
from jax.sharding import PartitionSpec as P

D = 2048
DRAFT = 4
CTX = 384
R_DEV = 8
EPS = 1e-05
THETA = 500000.0
NEGATIVE = -1e30


def shifted(array, axis, by):
    length = lax.axis_size(axis)
    pairs = [(i, i + by) for i in range(length) if 0 <= i + by < length]
    return lax.ppermute(array, axis, pairs)


def rotate(values, where_at):
    middle = values.shape[-1] // 2
    rates = jnp.exp(
        jnp.arange(middle, dtype=jnp.float32) * (-2.0 * math.log(THETA) / values.shape[-1])
    )
    angles = where_at.astype(jnp.float32)[..., None] * rates
    cosine = jnp.cos(angles)
    sine = jnp.sin(angles)
    first = values[..., :middle]
    second = values[..., middle:]
    return jnp.concatenate(
        [first * cosine - second * sine, second * cosine + first * sine], axis=-1
    )


def normalize(hidden, gain):
    wide = hidden.astype(jnp.float32)
    factor = lax.rsqrt(jnp.mean(wide * wide, axis=-1, keepdims=True) + EPS)
    return (wide * factor * gain).astype(jnp.bfloat16)


def attend(normed, lengths, cache, w_query, w_keyval, w_out):
    rows, drafts, width = normed.shape
    head_size = cache.shape[-1] // 2
    kv_count = cache.shape[2]
    q_count = w_query.shape[-1] // head_size
    group = q_count // kv_count
    flat = normed.reshape(rows * drafts, width)
    query = jnp.dot(flat, w_query, preferred_element_type=jnp.float32).reshape(
        rows, drafts, kv_count, group, head_size
    )
    keyval = jnp.dot(flat, w_keyval, preferred_element_type=jnp.float32).reshape(
        rows, drafts, kv_count, 2 * head_size
    )
    places = lengths[:, None] + jnp.arange(drafts, dtype=jnp.int32)[None, :]
    query = rotate(query, places[:, :, None, None]).astype(jnp.bfloat16)
    fresh_keys = rotate(keyval[..., :head_size], places[:, :, None]).astype(jnp.bfloat16)
    fresh_values = keyval[..., head_size:].astype(jnp.bfloat16)
    cached_keys = cache[..., :head_size]
    cached_values = cache[..., head_size:]
    scale = head_size ** (-0.5)
    old_scores = (
        jnp.einsum("rjkgd,rpkd->rkgjp", query, cached_keys, preferred_element_type=jnp.float32)
        * scale
    )
    live = jnp.arange(cache.shape[1], dtype=jnp.int32)[None, :] < lengths[:, None]
    old_scores = jnp.where(live[:, None, None, None, :], old_scores, NEGATIVE)
    new_scores = (
        jnp.einsum("rjkgd,rikd->rkgji", query, fresh_keys, preferred_element_type=jnp.float32)
        * scale
    )
    causal = jnp.arange(drafts)[None, :] <= jnp.arange(drafts)[:, None]
    new_scores = jnp.where(causal, new_scores, NEGATIVE)
    top = jnp.maximum(old_scores.max(axis=-1), new_scores.max(axis=-1))[..., None]
    old_weights = jnp.exp(old_scores - top)
    new_weights = jnp.exp(new_scores - top)
    total = old_weights.sum(axis=-1, keepdims=True) + new_weights.sum(axis=-1, keepdims=True)
    old_weights = (old_weights / total).astype(jnp.bfloat16)
    new_weights = (new_weights / total).astype(jnp.bfloat16)
    mixed = jnp.einsum(
        "rkgjp,rpkd->rjkgd", old_weights, cached_values, preferred_element_type=jnp.float32
    )
    mixed = mixed + jnp.einsum(
        "rkgji,rikd->rjkgd", new_weights, fresh_values, preferred_element_type=jnp.float32
    )
    heads_out = mixed.astype(jnp.bfloat16).reshape(rows * drafts, q_count * head_size)
    return jnp.dot(heads_out, w_out, preferred_element_type=jnp.float32)


def feed_forward(normed, gate_full, up_full, down_full):
    flat = normed.reshape(-1, normed.shape[-1])
    gate = jnp.dot(flat, gate_full, preferred_element_type=jnp.float32)
    up = jnp.dot(flat, up_full, preferred_element_type=jnp.float32)
    act = (jax.nn.silu(gate) * up).astype(jnp.bfloat16)
    return lax.dot_general(
        act, down_full, (((1,), (1,)), ((), ())), preferred_element_type=jnp.float32
    )


def local(
    exit_hidden,
    exit_depth,
    context_len,
    attn_gain,
    w_query,
    w_keyval,
    w_out,
    kv_cache,
    mlp_gain,
    w_gate,
    w_up,
    w_down,
):
    entry = lax.all_gather(exit_hidden, ("section", "tensor"), axis=2, tiled=True)
    gate_full, up_full, down_full = (
        lax.all_gather(w_gate[0], "dp", axis=0, tiled=True),
        lax.all_gather(w_up[0], "dp", axis=0, tiled=True),
        lax.all_gather(w_down[0], "dp", axis=0, tiled=True),
    )
    section = lax.axis_index("section")
    sections = lax.axis_size("section")
    pieces = 1
    members = R_DEV // pieces
    share = D // lax.axis_size("tensor")
    offset = lax.axis_index("tensor") * share
    entry = entry.reshape(pieces, members, DRAFT, D)
    depth = exit_depth.reshape(pieces, members)
    length = context_len.reshape(pieces, members)
    cache = kv_cache[0].reshape(pieces, members, CTX, kv_cache.shape[3], kv_cache.shape[4])
    gain = attn_gain[0]
    second_gain = mlp_gain[0]
    query_weight = w_query[0]
    keyval_weight = w_keyval[0]
    out_weight = w_out[0]

    def turn_step(turn, carry):
        received, outputs = carry
        block = turn - section
        valid = (block >= 0) & (block < pieces)
        index = jnp.clip(block, 0, pieces - 1)
        block_depth = depth[index]
        block_length = length[index]
        block_entry = entry[index]
        block_cache = cache[index]
        take = (block_depth >= section)[:, None, None]
        keep = (block_depth <= section)[:, None, None]
        active = valid & jnp.any(block_depth <= section)

        def compute(whole):
            return attend(
                normalize(whole, gain),
                block_length,
                block_cache,
                query_weight,
                keyval_weight,
                out_weight,
            )

        def branch_work(middle):
            return feed_forward(normalize(middle, second_gain), gate_full, up_full, down_full)

        def skipped(whole):
            return jnp.zeros((members * DRAFT, D), jnp.float32)

        whole = jnp.where(take, block_entry, received)
        partial_value = lax.cond(active, compute, skipped, whole)
        summed = lax.psum(partial_value, "tensor").reshape(members, DRAFT, D)
        middle = (whole.astype(jnp.float32) + summed).astype(jnp.bfloat16)
        branch = lax.cond(active, branch_work, skipped, middle)
        branch_sum = (
            lax.psum(branch.astype(jnp.bfloat16), "tensor")
            .astype(jnp.float32)
            .reshape(members, DRAFT, D)
        )
        updated = (middle.astype(jnp.float32) + branch_sum).astype(jnp.bfloat16)
        result = jnp.where(keep, updated, whole)
        own = lax.dynamic_slice_in_dim(result, offset, share, 2)
        stored = jnp.where(valid, own, outputs[index])
        outputs = lax.dynamic_update_index_in_dim(outputs, stored, index, 0)
        received = shifted(result, "section", 1)
        return (received, outputs)

    carried = D
    start = (
        jnp.zeros((members, DRAFT, carried), jnp.bfloat16),
        jnp.zeros((pieces, members, DRAFT, share), jnp.bfloat16),
    )
    final = lax.fori_loop(0, sections + pieces - 1, turn_step, start)
    return final[1]


def solution(mesh):
    in_specs = (
        P("dp", None, ("section", "tensor")),
        P("dp"),
        P("dp"),
        P("section", None),
        P("section", None, "tensor"),
        P("section", None, "tensor"),
        P("section", "tensor", None),
        P("section", "dp", None, "tensor", None),
        P("section", None),
        P("section", "dp", "tensor"),
        P("section", "dp", "tensor"),
        P("section", "dp", "tensor"),
    )
    out_specs = P("section", "dp", None, "tensor")
    return jax.shard_map(local, mesh=mesh, in_specs=in_specs, out_specs=out_specs, check_vma=False)
```

profile of v0, /device:TPU:0, one launch (start us, length us, event | category | flops | bytes accessed | tf_op | source)
XLA Modules:
  0.0 562.1 jit_solution(6729195397710734736)
XLA Ops:
  8.8 6.6 %copy.31 = bf16[1,2048,1024]{1,2,0:T(8,128)(2,1)} copy(bf16[1,2048,1024]{2,1,0:T(8,128)(2,1)} %param.22) | data formatting | bytes 8388608 | tf_op args[4]
  15.4 3.5 copy.33
  19.0 3.1 copy.32
  22.0 10.8 %all_gather.12 = bf16[8,4,2048]{2,1,0:T(4,128)(2,1)S(1)} all-gather(bf16[8,4,512]{2,1,0:T(4,128)(2,1)S(1)} %copy-done.7), channel_id=1, replica_groups=mesh['section'=2,'tensor'=2,'dp'=8] {'section','tensor'}, dimensions={2}, use_global_device_ids=true | all-gather | bytes 163840 | tf_op jit(solution)/shard_map/all_gather | solution.py:115
  33.5 103.2 %all-gather.7.cloned.1.call-done = bf16[1,2048,2048]{2,1,0:T(8,128)(2,1)} async-done(((bf16[1,256,2048]{2,1,0:T(8,128)(2,1)}), bf16[1,2048,2048]{2,1,0:T(8,128)(2,1)}) %all-gather.7.cloned.1.call-update) | async-done | bytes 8388624 | tf_op jit(solution)/shard_map/all_gather | solution.py:117
  136.7 124.8 %all-gather.9.cloned.1.call-done = bf16[1,2048,2048]{2,1,0:T(8,128)(2,1)} async-done(((bf16[1,256,2048]{2,1,0:T(8,128)(2,1)}), bf16[1,2048,2048]{2,1,0:T(8,128)(2,1)}) %all-gather.9.cloned.1.call-update) | async-done | bytes 8388624 | tf_op jit(solution)/shard_map/all_gather | solution.py:118
  261.5 124.8 %all-gather.11.cloned.1.call-done = bf16[1,2048,2048]{2,1,0:T(8,128)(2,1)} async-done(((bf16[1,256,2048]{2,1,0:T(8,128)(2,1)}), bf16[1,2048,2048]{2,1,0:T(8,128)(2,1)}) %all-gather.11.cloned.1.call-update) | async-done | bytes 8388624 | tf_op jit(solution)/shard_map/all_gather | solution.py:119
  386.4 168.3 %while.18 = (s32[]{:T(128)}, bf16[8,4,2048]{2,1,0:T(4,128)(2,1)S(1)}, bf16[1,8,4,1024]{3,2,1,0:T(4,128)(2,1)S(1)}, s32[]{:T(128)}, s32[1,8]{1,0:T(1,128)S(1)}, /...) while((s32[]{:T(128)}, ...), condition=%wide.region_14.15_spmd, body=%wide.region_1.14_spmd.sunk | while | flops 1196018816 | bytes 63734276 | solution.py:189
  387.9 17.9 %conditional.4 = (f32[32,2048]{1,0:T(8,128)S(1)}) conditional(s32[]{:T(128)} %convert_element_type.166, () %tuple.68, (s32[1,8]{1,0:T(1,128)}, bf16[8,4,2048]{2,1,0:T(4,128)(2,1)S(1)}, f32[1,2048]{1,0:T(1,128)S(1)}, bf16[2048,1024]{0,1:T(8,128)(2,1)}, bf16[1,8,384,4,128]{2,4,3,1,0:T(8,128)(2,1)}, /*index=5*/bf16[2048,512]{0,1:T(8,128)(2,1)S(1)}, ...), branch_computations={%region_2.2_spmd, %region_3.8_spmd} | conditional | flops 389106816 | bytes 31677728 | solution.py:167
  389.9 4.4 fusion.18
  394.5 1.3 fusion.42
  398.2 1.6 copy.28
  400.1 2.1 fusion.8
  402.7 3.0 fusion.44
  406.6 21.6 %all-reduce.3.cloned.1.call-done = f32[8,4,2048]{2,1,0:T(4,128)} async-done(((f32[8,4,2048]{2,1,0:T(4,128)}), f32[8,4,2048]{2,1,0:T(4,128)}) %all-reduce.3.cloned.1.call-update) | async-done | bytes 262160 | tf_op jit(solution)/shard_map/while/body/eval_jaxpr/psum | solution.py:168
  429.2 15.1 %conditional.5 = (bf16[32,2048]{1,0:T(8,128)(2,1)S(1)}) conditional(s32[]{:T(128)} %convert_element_type.166, () %tuple.67, (bf16[8,4,2048]{2,1,0:T(4,128)(2,1)S(1)}, f32[1,2048]{1,0:T(1,128)S(1)}, bf16[2048,2048]{1,0:T(8,128)(2,1)}, bf16[2048,2048]{1,0:T(8,128)(2,1)}, bf16[2048,2048]{1,0:T(8,128)(2,1)}) %tuple.70), branch_computations={%region_10.10_spmd, %region_11.12_spmd} | conditional | flops 806158336 | bytes 26747400 | solution.py:170
  429.6 4.9 fusion.43
  434.5 9.8 %fusion.28 = bf16[32,2048]{1,0:T(8,128)(2,1)S(1)} fusion(bf16[2048,2048]{1,0:T(8,128)(2,1)} %get-tuple-element.508, bf16[32,2048]{1,0:T(8,128)(2,1)S(1)} %reshape.208, bf16[2048,2048]{1,0:T(8,128)(2,1)} %get-tuple-element.507, f32[32,2048]{1,0:T(8,128)S(1)} %fusion.43), kind=kOutput, calls=%fused_computation.51 | convolution fusion | flops 537264128 | bytes 17301504 | tf_op jit(solution)/shard_map/while/body/eval_jaxpr/cond/branch_1_fun/dot_general | solution.py:96
  445.1 21.7 %all-reduce.5.cloned.1.call-done = bf16[8,4,2048]{2,1,0:T(4,128)(2,1)} async-done(((bf16[8,4,2048]{2,1,0:T(4,128)(2,1)}), bf16[8,4,2048]{2,1,0:T(4,128)(2,1)}) %all-reduce.5.cloned.1.call-update) | async-done | bytes 131088 | tf_op jit(solution)/shard_map/while/body/eval_jaxpr/psum | solution.py:172
  466.8 1.1 fusion.57
  467.9 1.3 collective-permute-start
  472.5 41.3 %all-reduce.3.cloned.1.call-done = f32[8,4,2048]{2,1,0:T(4,128)} async-done(((f32[8,4,2048]{2,1,0:T(4,128)}), f32[8,4,2048]{2,1,0:T(4,128)}) %all-reduce.3.cloned.1.call-update) | async-done | bytes 262160 | tf_op jit(solution)/shard_map/while/body/eval_jaxpr/psum | solution.py:168
  515.6 35.7 %all-reduce.5.cloned.1.call-done = bf16[8,4,2048]{2,1,0:T(4,128)(2,1)} async-done(((bf16[8,4,2048]{2,1,0:T(4,128)(2,1)}), bf16[8,4,2048]{2,1,0:T(4,128)(2,1)}) %all-reduce.5.cloned.1.call-update) | async-done | bytes 131088 | tf_op jit(solution)/shard_map/while/body/eval_jaxpr/psum | solution.py:172
  552.4 1.3 collective-permute-start
  (87 shorter events, 19.2 us)
Async XLA Ops:
  6.5 130.2 %all-gather.7.cloned.1.call-start = ((), (), s32[]{:S(2)}) async-start(), calls=%async_computation | async-start | bytes 9437184 | tf_op jit(solution)/shard_map/all_gather | solution.py:117
  7.3 254.2 %all-gather.9.cloned.1.call-start = ((), (), s32[]{:S(2)}) async-start(), calls=%async_computation.1 | async-start | bytes 9437184 | tf_op jit(solution)/shard_map/all_gather | solution.py:118
  8.0 378.3 %all-gather.11.cloned.1.call-start = ((), (), s32[]{:S(2)}) async-start(), calls=%async_computation.2 | async-start | bytes 9437184 | tf_op jit(solution)/shard_map/all_gather | solution.py:119
  8.8 6.7 %copy-start.1 = (bf16[1,8,384,4,128]{4,3,2,1,0:T(4,128)(2,1)S(1)}, bf16[1,8,384,4,128]{4,3,2,1,0:T(4,128)(2,1)}, u32[]{:S(2)}) copy-start(bf16[1,8,384,4,128]{4,3,2,1,0:T(4,128)(2,1)} %param.25) | copy-start | bytes 9437188
  15.4 6.6 %copy-start.7 = (bf16[8,4,512]{2,1,0:T(4,128)(2,1)S(1)}, bf16[8,4,512]{2,1,0:T(4,128)(2,1)}, u32[]{:S(2)}) copy-start(bf16[8,4,512]{2,1,0:T(4,128)(2,1)} %param.18) | copy-start | bytes 98308
  15.4 17.4 %copy-start.8 = (s32[8]{0:T(128)S(1)}, s32[8]{0:T(128)}, u32[]{:S(2)}) copy-start(s32[8]{0:T(128)} %param.19) | copy-start | bytes 100
  15.4 371.0 %copy-start.4 = (f32[1,2048]{1,0:T(1,128)S(1)}, f32[1,2048]{1,0:T(1,128)}, u32[]{:S(2)}) copy-start(f32[1,2048]{1,0:T(1,128)} %param.21) | copy-start | bytes 24580
  15.4 371.0 %copy-start.5 = (f32[1,2048]{1,0:T(1,128)S(1)}, f32[1,2048]{1,0:T(1,128)}, u32[]{:S(2)}) copy-start(f32[1,2048]{1,0:T(1,128)} %param.26) | copy-start | bytes 24580
  386.4 41.8 %all-reduce.3.cloned.1.call-start = ((), (), s32[]{:S(2)}) async-start(), calls=%async_computation.3 | async-start | bytes 524288 | tf_op jit(solution)/shard_map/while/body/eval_jaxpr/psum | solution.py:168
  389.9 6.7 %copy-start.2 = (bf16[1,8,384,4,128]{2,4,3,1,0:T(8,128)(2,1)S(1)}, bf16[1,8,384,4,128]{2,4,3,1,0:T(8,128)(2,1)}, u32[]{:S(2)}) copy-start(bf16[1,8,384,4,128]{2,4,3,1,0:T(8,128)(2,1)} %get-tuple-element.501) | copy-start | bytes 9437188 | tf_op jit(solution)/shard_map/while/body/eval_jaxpr/cond
  399.7 2.6 copy-start
  406.6 60.2 %all-reduce.5.cloned.1.call-start = ((), (), s32[]{:S(2)}) async-start(), calls=%async_computation.4 | async-start | bytes 262144 | tf_op jit(solution)/shard_map/while/body/eval_jaxpr/psum | solution.py:172
  429.2 37.6 %copy-start.6 = (pred[8]{0:T(512)(128)(4,1)S(1)}, pred[8]{0:T(512)(128)(4,1)}, u32[]{:S(2)}) copy-start(pred[8]{0:T(512)(128)(4,1)} %get-tuple-element.740) | copy-start | bytes 28 | tf_op jit(solution)/shard_map/while
  429.2 40.9 %copy-start.9 = (s32[8]{0:T(128)S(1)}, s32[8]{0:T(128)}, u32[]{:S(2)}) copy-start(s32[8]{0:T(128)} %get-tuple-element.865) | copy-start | bytes 100 | tf_op jit(solution)/shard_map/while
  467.9 2.3 collective-permute-start
  470.2 43.6 %all-reduce.3.cloned.1.call-start = ((), (), s32[]{:S(2)}) async-start(), calls=%async_computation.3 | async-start | bytes 524288 | tf_op jit(solution)/shard_map/while/body/eval_jaxpr/psum | solution.py:168
  472.4 78.9 %all-reduce.5.cloned.1.call-start = ((), (), s32[]{:S(2)}) async-start(), calls=%async_computation.4 | async-start | bytes 262144 | tf_op jit(solution)/shard_map/while/body/eval_jaxpr/psum | solution.py:172
  514.8 36.5 %copy-start.6 = (pred[8]{0:T(512)(128)(4,1)S(1)}, pred[8]{0:T(512)(128)(4,1)}, u32[]{:S(2)}) copy-start(pred[8]{0:T(512)(128)(4,1)} %get-tuple-element.740) | copy-start | bytes 28 | tf_op jit(solution)/shard_map/while
  514.8 39.9 %copy-start.9 = (s32[8]{0:T(128)S(1)}, s32[8]{0:T(128)}, u32[]{:S(2)}) copy-start(s32[8]{0:T(128)} %get-tuple-element.865) | copy-start | bytes 100 | tf_op jit(solution)/shard_map/while
  552.4 2.3 collective-permute-start
  554.7 0.6 copy-start.3
Sparse Core Ops, SparseCore 0:
  9.5 127.1 all-gather.6
  138.8 122.6 all-gather.8
  263.6 122.6 all-gather.10
  406.7 21.4 all-reduce.2
  445.2 21.5 all-reduce.4
  472.9 40.7 all-reduce.2
  516.0 35.2 all-reduce.4
where the time goes:
time: 563 us; the launch traced here: 562 us
  waiting for transfers between devices  477 us (85%)
  matrix products  27 us (5%)
  local copies, waits for them, and re-layouts  18.9 us (3%)
  between operations  13.5 us (2%)
  blocking collectives  10.8 us (2%)
  other arithmetic  10.5 us (2%)
    all_gather x1, waiting for transfers between devices, local(): lax.all_gather(w_down[0], 'dp', axis=0, tiled=True)  125 us
    all_gather x1, waiting for transfers between devices, local(): lax.all_gather(w_up[0], 'dp', axis=0, tiled=True)  125 us
    all_gather x1, waiting for transfers between devices, local(): lax.all_gather(w_gate[0], 'dp', axis=0, tiled=True)  103 us
    psum x2, waiting for transfers between devices, turn_step(): summed = lax.psum(partial_value, 'tensor').reshape(members, DRAFT, D)  62.8 us
    psum x2, waiting for transfers between devices, turn_step(): lax.psum(branch.astype(jnp.bfloat16), 'tensor').astype(jnp.float32)  57.4 us
  transfers between devices with their start and end apart: 9, of which 9 were waited for; matrix products, arithmetic and copies ran while one was open for 2% of the time, Pallas kernels for 0%

commit v1 on v0

--- a/solution.py
+++ b/solution.py
@@ -165,7 +165,7 @@
 
         whole = jnp.where(take, block_entry, received)
         partial_value = lax.cond(active, compute, skipped, whole)
-        summed = lax.psum(partial_value, "tensor").reshape(members, DRAFT, D)
+        summed = jnp.sum(lax.all_gather(partial_value, "tensor"), axis=0).reshape(members, DRAFT, D)
         middle = (whole.astype(jnp.float32) + summed).astype(jnp.bfloat16)
         branch = lax.cond(active, branch_work, skipped, middle)
         branch_sum = (

time: 563 us -> 526 us (0.934)
  waiting for transfers between devices: 477 us -> 430 us
  blocking collectives: 10.8 us -> 24.9 us
    psum x2 -> x0, waiting for transfers between devices: 62.8 us -> none  [turn_step(): summed = lax.psum(partial_value, 'tensor').reshape(members, DRAFT, D)]
    psum x2, waiting for transfers between devices: 57.4 us -> 73.3 us  [turn_step(): lax.psum(branch.astype(jnp.bfloat16), 'tensor').astype(jnp.float32)]
    all_gather x0 -> x2, blocking collectives: none -> 14.1 us  [turn_step(): lax.all_gather(partial_value, 'tensor')]
  transfers between devices with their start and end apart: 9 -> 7, of which waited for: 9 -> 7; matrix products, arithmetic and copies ran while one was open for 2% -> 3% of each run, Pallas kernels for 0% -> 0%
where the time goes in v1:
time: 526 us
  waiting for transfers between devices  430 us (82%)
  matrix products  27 us (5%)
  blocking collectives  24.9 us (5%)
  local copies, waits for them, and re-layouts  17.4 us (3%)
  between operations  13.2 us (3%)
  other arithmetic  8.6 us (2%)
    all_gather x1, waiting for transfers between devices, local(): lax.all_gather(w_down[0], 'dp', axis=0, tiled=True)  125 us
    all_gather x1, waiting for transfers between devices, local(): lax.all_gather(w_up[0], 'dp', axis=0, tiled=True)  125 us
    all_gather x1, waiting for transfers between devices, local(): lax.all_gather(w_gate[0], 'dp', axis=0, tiled=True)  103 us
    psum x2, waiting for transfers between devices, turn_step(): lax.psum(branch.astype(jnp.bfloat16), 'tensor').astype(jnp.float32)  73.3 us
    all_gather x2, blocking collectives, turn_step(): lax.all_gather(partial_value, 'tensor')  14.1 us
    all_gather x1, blocking collectives, local(): lax.all_gather(exit_hidden, ('section', 'tensor'), axis=2, tiled=True)  10.8 us
  transfers between devices with their start and end apart: 7, of which 7 were waited for; matrix products, arithmetic and copies ran while one was open for 3% of the time, Pallas kernels for 0%

profile of v1, /device:TPU:0, one launch (start us, length us, event | category | flops | bytes accessed | tf_op | source)
XLA Modules:
  0.0 525.5 jit_solution(9696177000326557575)
XLA Ops:
  8.8 6.6 %copy.31 = bf16[1,2048,1024]{1,2,0:T(8,128)(2,1)} copy(bf16[1,2048,1024]{2,1,0:T(8,128)(2,1)} %param.22) | data formatting | bytes 8388608 | tf_op args[4]
  15.4 3.5 copy.33
  18.9 3.1 copy.32
  22.0 10.8 %all_gather.32 = bf16[8,4,2048]{2,1,0:T(4,128)(2,1)S(1)} all-gather(bf16[8,4,512]{2,1,0:T(4,128)(2,1)S(1)} %copy-done.7), channel_id=1, replica_groups=mesh['section'=2,'tensor'=2,'dp'=8] {'section','tensor'}, dimensions={2}, use_global_device_ids=true | all-gather | bytes 163840 | tf_op jit(solution)/shard_map/all_gather | solution.py:115
  33.5 103.2 %all-gather.10.cloned.1.call-done = bf16[1,2048,2048]{2,1,0:T(8,128)(2,1)} async-done(((bf16[1,256,2048]{2,1,0:T(8,128)(2,1)}), bf16[1,2048,2048]{2,1,0:T(8,128)(2,1)}) %all-gather.10.cloned.1.call-update) | async-done | bytes 8388624 | tf_op jit(solution)/shard_map/all_gather | solution.py:117
  136.7 124.8 %all-gather.12.cloned.1.call-done = bf16[1,2048,2048]{2,1,0:T(8,128)(2,1)} async-done(((bf16[1,256,2048]{2,1,0:T(8,128)(2,1)}), bf16[1,2048,2048]{2,1,0:T(8,128)(2,1)}) %all-gather.12.cloned.1.call-update) | async-done | bytes 8388624 | tf_op jit(solution)/shard_map/all_gather | solution.py:118
  261.5 124.8 %all-gather.14.cloned.1.call-done = bf16[1,2048,2048]{2,1,0:T(8,128)(2,1)} async-done(((bf16[1,256,2048]{2,1,0:T(8,128)(2,1)}), bf16[1,2048,2048]{2,1,0:T(8,128)(2,1)}) %all-gather.14.cloned.1.call-update) | async-done | bytes 8388624 | tf_op jit(solution)/shard_map/all_gather | solution.py:119
  386.4 132.0 %while.18 = (s32[]{:T(128)}, bf16[8,4,2048]{2,1,0:T(4,128)(2,1)S(1)}, bf16[1,8,4,1024]{3,2,1,0:T(4,128)(2,1)S(1)}, s32[]{:T(128)}, s32[1,8]{1,0:T(1,128)S(1)}, /...) while((s32[]{:T(128)}, ...), condition=%wide.region_14.15_spmd, body=%wide.region_1.14_spmd.sunk | while | flops 1196018816 | bytes 63734248 | solution.py:189
  387.9 17.9 %conditional.4 = (f32[32,2048]{1,0:T(8,128)S(1)}) conditional(s32[]{:T(128)} %convert_element_type.166, () %tuple.68, (s32[1,8]{1,0:T(1,128)}, bf16[8,4,2048]{2,1,0:T(4,128)(2,1)S(1)}, f32[1,2048]{1,0:T(1,128)S(1)}, bf16[2048,1024]{0,1:T(8,128)(2,1)}, bf16[1,8,384,4,128]{2,4,3,1,0:T(8,128)(2,1)}, /*index=5*/bf16[2048,512]{0,1:T(8,128)(2,1)S(1)}, ...), branch_computations={%region_2.2_spmd, %region_3.8_spmd} | conditional | flops 389106816 | bytes 31677728 | solution.py:167
  389.9 4.4 fusion.18
  394.5 1.3 fusion.42
  398.2 1.6 copy.28
  400.1 2.1 fusion.8
  402.7 3.0 fusion.44
  405.7 7.0 %all-gather.5 = f32[64,2048]{1,0:T(8,128)S(1)} all-gather(f32[32,2048]{1,0:T(8,128)S(1)} %get-tuple-element.804), channel_id=2, replica_groups=mesh['section'=2,'tensor'=2,'dp'=8] {'tensor'}, dimensions={0}, use_global_device_ids=true | all-gather | bytes 786432 | tf_op jit(solution)/shard_map/while/body/eval_jaxpr/all_gather | solution.py:168
  413.0 15.1 %conditional.5 = (bf16[32,2048]{1,0:T(8,128)(2,1)S(1)}) conditional(s32[]{:T(128)} %convert_element_type.166, () %tuple.67, (bf16[8,4,2048]{2,1,0:T(4,128)(2,1)S(1)}, f32[1,2048]{1,0:T(1,128)S(1)}, bf16[2048,2048]{1,0:T(8,128)(2,1)}, bf16[2048,2048]{1,0:T(8,128)(2,1)}, bf16[2048,2048]{1,0:T(8,128)(2,1)}) %tuple.70), branch_computations={%region_10.10_spmd, %region_11.12_spmd} | conditional | flops 806158336 | bytes 26747400 | solution.py:170
  413.4 4.9 fusion.43
  418.3 9.8 %fusion.28 = bf16[32,2048]{1,0:T(8,128)(2,1)S(1)} fusion(bf16[2048,2048]{1,0:T(8,128)(2,1)} %get-tuple-element.508, bf16[32,2048]{1,0:T(8,128)(2,1)S(1)} %reshape.208, bf16[2048,2048]{1,0:T(8,128)(2,1)} %get-tuple-element.507, f32[32,2048]{1,0:T(8,128)S(1)} %fusion.43), kind=kOutput, calls=%fused_computation.51 | convolution fusion | flops 537264128 | bytes 17301504 | tf_op jit(solution)/shard_map/while/body/eval_jaxpr/cond/branch_1_fun/dot_general | solution.py:96
  428.9 19.9 %all-reduce.2.cloned.1.call-done = bf16[8,4,2048]{2,1,0:T(4,128)(2,1)} async-done(((bf16[8,4,2048]{2,1,0:T(4,128)(2,1)}), bf16[8,4,2048]{2,1,0:T(4,128)(2,1)}) %all-reduce.2.cloned.1.call-update) | async-done | bytes 131088 | tf_op jit(solution)/shard_map/while/body/eval_jaxpr/psum | solution.py:172
  448.7 1.1 fusion.57
  449.8 1.3 collective-permute-start
  453.5 7.0 %all-gather.5 = f32[64,2048]{1,0:T(8,128)S(1)} all-gather(f32[32,2048]{1,0:T(8,128)S(1)} %get-tuple-element.804), channel_id=2, replica_groups=mesh['section'=2,'tensor'=2,'dp'=8] {'tensor'}, dimensions={0}, use_global_device_ids=true | all-gather | bytes 786432 | tf_op jit(solution)/shard_map/while/body/eval_jaxpr/all_gather | solution.py:168
  461.6 53.5 %all-reduce.2.cloned.1.call-done = bf16[8,4,2048]{2,1,0:T(4,128)(2,1)} async-done(((bf16[8,4,2048]{2,1,0:T(4,128)(2,1)}), bf16[8,4,2048]{2,1,0:T(4,128)(2,1)}) %all-reduce.2.cloned.1.call-update) | async-done | bytes 131088 | tf_op jit(solution)/shard_map/while/body/eval_jaxpr/psum | solution.py:172
  516.1 1.3 collective-permute-start
  (85 shorter events, 15.8 us)
Async XLA Ops:
  6.5 130.2 %all-gather.10.cloned.1.call-start = ((), (), s32[]{:S(2)}) async-start(), calls=%async_computation | async-start | bytes 9437184 | tf_op jit(solution)/shard_map/all_gather | solution.py:117
  7.3 254.2 %all-gather.12.cloned.1.call-start = ((), (), s32[]{:S(2)}) async-start(), calls=%async_computation.1 | async-start | bytes 9437184 | tf_op jit(solution)/shard_map/all_gather | solution.py:118
  8.0 378.3 %all-gather.14.cloned.1.call-start = ((), (), s32[]{:S(2)}) async-start(), calls=%async_computation.2 | async-start | bytes 9437184 | tf_op jit(solution)/shard_map/all_gather | solution.py:119
  8.8 6.6 %copy-start.1 = (bf16[1,8,384,4,128]{4,3,2,1,0:T(4,128)(2,1)S(1)}, bf16[1,8,384,4,128]{4,3,2,1,0:T(4,128)(2,1)}, u32[]{:S(2)}) copy-start(bf16[1,8,384,4,128]{4,3,2,1,0:T(4,128)(2,1)} %param.25) | copy-start | bytes 9437188
  15.4 6.6 %copy-start.7 = (bf16[8,4,512]{2,1,0:T(4,128)(2,1)S(1)}, bf16[8,4,512]{2,1,0:T(4,128)(2,1)}, u32[]{:S(2)}) copy-start(bf16[8,4,512]{2,1,0:T(4,128)(2,1)} %param.18) | copy-start | bytes 98308
  15.4 17.5 %copy-start.8 = (s32[8]{0:T(128)S(1)}, s32[8]{0:T(128)}, u32[]{:S(2)}) copy-start(s32[8]{0:T(128)} %param.19) | copy-start | bytes 100
  15.4 371.0 %copy-start.4 = (f32[1,2048]{1,0:T(1,128)S(1)}, f32[1,2048]{1,0:T(1,128)}, u32[]{:S(2)}) copy-start(f32[1,2048]{1,0:T(1,128)} %param.21) | copy-start | bytes 24580
  15.4 371.0 %copy-start.5 = (f32[1,2048]{1,0:T(1,128)S(1)}, f32[1,2048]{1,0:T(1,128)}, u32[]{:S(2)}) copy-start(f32[1,2048]{1,0:T(1,128)} %param.26) | copy-start | bytes 24580
  386.4 62.3 %all-reduce.2.cloned.1.call-start = ((), (), s32[]{:S(2)}) async-start(), calls=%async_computation.3 | async-start | bytes 262144 | tf_op jit(solution)/shard_map/while/body/eval_jaxpr/psum | solution.py:172
  389.9 6.7 %copy-start.2 = (bf16[1,8,384,4,128]{2,4,3,1,0:T(8,128)(2,1)S(1)}, bf16[1,8,384,4,128]{2,4,3,1,0:T(8,128)(2,1)}, u32[]{:S(2)}) copy-start(bf16[1,8,384,4,128]{2,4,3,1,0:T(8,128)(2,1)} %get-tuple-element.501) | copy-start | bytes 9437188 | tf_op jit(solution)/shard_map/while/body/eval_jaxpr/cond
  399.7 2.6 copy-start
  413.0 35.7 %copy-start.6 = (pred[8]{0:T(512)(128)(4,1)S(1)}, pred[8]{0:T(512)(128)(4,1)}, u32[]{:S(2)}) copy-start(pred[8]{0:T(512)(128)(4,1)} %get-tuple-element.740) | copy-start | bytes 28 | tf_op jit(solution)/shard_map/while
  413.0 39.1 %copy-start.9 = (s32[8]{0:T(128)S(1)}, s32[8]{0:T(128)}, u32[]{:S(2)}) copy-start(s32[8]{0:T(128)} %get-tuple-element.866) | copy-start | bytes 100 | tf_op jit(solution)/shard_map/while
  449.8 2.3 collective-permute-start
  452.1 62.9 %all-reduce.2.cloned.1.call-start = ((), (), s32[]{:S(2)}) async-start(), calls=%async_computation.3 | async-start | bytes 262144 | tf_op jit(solution)/shard_map/while/body/eval_jaxpr/psum | solution.py:172
  460.8 54.2 %copy-start.6 = (pred[8]{0:T(512)(128)(4,1)S(1)}, pred[8]{0:T(512)(128)(4,1)}, u32[]{:S(2)}) copy-start(pred[8]{0:T(512)(128)(4,1)} %get-tuple-element.740) | copy-start | bytes 28 | tf_op jit(solution)/shard_map/while
  460.8 57.6 %copy-start.9 = (s32[8]{0:T(128)S(1)}, s32[8]{0:T(128)}, u32[]{:S(2)}) copy-start(s32[8]{0:T(128)} %get-tuple-element.866) | copy-start | bytes 100 | tf_op jit(solution)/shard_map/while
  516.1 2.3 collective-permute-start
  518.4 0.6 copy-start.3
Sparse Core Ops, SparseCore 0:
  9.5 127.1 all-gather.9
  138.8 122.6 all-gather.11
  263.6 122.6 all-gather.13
  429.0 19.7 all-reduce.1
  461.7 53.2 all-reduce.1
